TPU v7x, 128 devices: a whole 4x4x4 slice. The times are simulated.
128 devices in a mesh: sx: 8 (over y, core), sy: 16 (over z, x).
Axes of the slice: x: 4, y: 4, z: 4, core: 2. Of those that a mesh axis runs over, the one named last changes fastest.
Arguments:
- features: bfloat16 [131072, 384], P(('sx', 'sy'))
- cotangent: bfloat16 [131072, 384], P(('sx', 'sy')), may hold values from -6 to 6
- hilbert_rank: int32 [131072], P(('sx', 'sy')), may hold values from 0 to 131071, as said below
- w_qkv: bfloat16 [384, 1152], replicated
- w_proj: bfloat16 [384, 384], replicated, may hold values from -0.3125 to 0.3125
Outputs:
- outputs: bfloat16 [131072, 384], P(('sx', 'sy'))
- grad_features: bfloat16 [131072, 384], P(('sx', 'sy'))
- grad_qkv: float32 [384, 1152], replicated
- grad_proj: float32 [384, 384], replicated
Inputs may be any that keep to these rules, and one draw needn't show every extreme that they name: hilbert_rank is a permutation. Hilbert positions t * 1024 to (t + 1) * 1024 - 1 belong to device t. Every device sends rows to every device, 4 to 16 rows to each, and every device has 16 rows for some owners and receives 16 rows from some devices.
All inputs are finite; a program needn't handle non-finite values.
Results may differ from a plain program's by a relative error of at most 0.004.
The roundings to bfloat16 on the way count: a program that leaves them out, or rounds other values in their place, can miss the bound.
Values may be sent and summed in bfloat16 or wider, within the bound.
A program may use at most 64 MiB of HBM per device.

v0:
```python
import math
import jax
import jax.numpy as jnp
from jax import lax
from jax.sharding import PartitionSpec as P

HEADS = 24
PATCH = 1024


def contract(left_op, right_op, left_dim, right_dim):
    return lax.dot_general(
        left_op,
        right_op,
        (((left_dim,), (right_dim,)), ((), ())),
        preferred_element_type=jnp.float32,
    )


def head_pass(query_rows, key_rows, value_rows, grad_slice):
    score_scale = query_rows.shape[1] ** (-0.5)
    scores = contract(query_rows, key_rows, 1, 1) * score_scale
    shifted = jnp.exp(scores - jnp.max(scores, axis=1, keepdims=True))
    prob_full = shifted / jnp.sum(shifted, axis=1, keepdims=True)
    prob_low = prob_full.astype(jnp.bfloat16)
    attended = jnp.dot(prob_low, value_rows, preferred_element_type=jnp.float32).astype(
        jnp.bfloat16
    )
    dprobs = contract(grad_slice, value_rows, 1, 1)
    dscores = (
        prob_full * (dprobs - jnp.sum(dprobs * prob_full, axis=1, keepdims=True)) * score_scale
    ).astype(jnp.bfloat16)
    dquery = jnp.dot(dscores, key_rows, preferred_element_type=jnp.float32).astype(jnp.bfloat16)
    dkey_rows = contract(dscores, query_rows, 0, 0).astype(jnp.bfloat16)
    dvalue = contract(prob_low, grad_slice, 0, 0).astype(jnp.bfloat16)
    return (attended, dquery, dkey_rows, dvalue)


def patch_pass(block_rows, block_grads, w_qkv, w_proj, head_count):
    feat_width = block_rows.shape[1]
    head_dim = feat_width // head_count
    values = block_rows.astype(jnp.float32)
    row_mean = jnp.mean(values, axis=1, keepdims=True)
    centred = values - row_mean
    inv_std = lax.rsqrt(jnp.mean(centred * centred, axis=1, keepdims=True) + 1e-05)
    normed = centred * inv_std
    normed_low = normed.astype(jnp.bfloat16)
    projected = jnp.dot(normed_low, w_qkv, preferred_element_type=jnp.float32).astype(jnp.bfloat16)
    upstream = contract(block_grads, w_proj, 1, 1).astype(jnp.bfloat16)

    def one_head(head_index):
        head_start = head_index * head_dim
        query_rows = lax.dynamic_slice_in_dim(projected, head_start, head_dim, 1)
        key_rows = lax.dynamic_slice_in_dim(projected, head_start + feat_width, head_dim, 1)
        value_rows = lax.dynamic_slice_in_dim(projected, head_start + 2 * feat_width, head_dim, 1)
        grad_slice = lax.dynamic_slice_in_dim(upstream, head_start, head_dim, 1)
        return head_pass(query_rows, key_rows, value_rows, grad_slice)

    heads_out = lax.map(one_head, jnp.arange(head_count, dtype=jnp.int32))

    def merge_heads(stacked):
        return jnp.transpose(stacked, (1, 0, 2)).reshape(stacked.shape[1], feat_width)

    attended = merge_heads(heads_out[0])
    dprojected = jnp.concatenate(
        [merge_heads(heads_out[1]), merge_heads(heads_out[2]), merge_heads(heads_out[3])], axis=1
    )
    mixed_out = jnp.dot(attended, w_proj, preferred_element_type=jnp.float32)
    output = (values + mixed_out).astype(jnp.bfloat16)
    dnormed = contract(dprojected, w_qkv, 1, 1)
    dnorm_mean = jnp.mean(dnormed, axis=1, keepdims=True)
    cross_mean = jnp.mean(dnormed * normed, axis=1, keepdims=True)
    dinput = inv_std * (dnormed - dnorm_mean - normed * cross_mean)
    grad_input = (block_grads.astype(jnp.float32) + dinput).astype(jnp.bfloat16)
    return (output, grad_input, normed_low, dprojected, attended)


def on_device(features, cotangent, hilbert_rank, w_qkv, w_proj):
    row_count = features.shape[0]
    feat_width = features.shape[1]
    size_x = lax.axis_size("sx")
    size_y = lax.axis_size("sy")
    devices = size_x * size_y
    capacity = 2 * row_count // devices
    slot_total = devices * capacity
    owner_dev = hilbert_rank // row_count
    place_row = hilbert_rank % row_count
    sort_order = jnp.argsort(hilbert_rank)
    owner_sorted = owner_dev[sort_order]
    labels = jnp.arange(devices, dtype=jnp.int32)
    counts = jnp.sum((owner_dev[:, None] == labels[None, :]).astype(jnp.int32), axis=0)
    starts = jnp.cumsum(counts) - counts
    first_slot = jnp.sum(
        jnp.where(owner_sorted[:, None] == labels[None, :], starts[None, :], 0), axis=1
    )
    slot_sorted = owner_sorted * capacity + jnp.arange(row_count, dtype=jnp.int32) - first_slot
    slot_index = jnp.zeros((row_count,), jnp.int32).at[sort_order].set(slot_sorted)
    send_rows = jnp.zeros((slot_total, feat_width), features.dtype).at[slot_index].set(features)
    send_grads = jnp.zeros((slot_total, feat_width), cotangent.dtype).at[slot_index].set(cotangent)
    send_place = jnp.full((slot_total,), row_count, jnp.int32).at[slot_index].set(place_row)
    got_rows, got_grads, got_place = (
        lax.all_to_all(send_rows, ("sx", "sy"), split_axis=0, concat_axis=0, tiled=True),
        lax.all_to_all(send_grads, ("sx", "sy"), split_axis=0, concat_axis=0, tiled=True),
        lax.all_to_all(send_place, ("sx", "sy"), split_axis=0, concat_axis=0, tiled=True),
    )
    curve_rows = (
        jnp.zeros((row_count, feat_width), jnp.bfloat16).at[got_place].set(got_rows, mode="drop")
    )
    curve_grads = (
        jnp.zeros((row_count, feat_width), jnp.bfloat16).at[got_place].set(got_grads, mode="drop")
    )
    patch_total = row_count // PATCH

    def run_patch(both_blocks):
        return patch_pass(both_blocks[0], both_blocks[1], w_qkv, w_proj, HEADS)

    results = lax.map(
        run_patch,
        (
            curve_rows.reshape(patch_total, PATCH, feat_width),
            curve_grads.reshape(patch_total, PATCH, feat_width),
        ),
    )
    curve_out = results[0].reshape(row_count, feat_width)
    curve_grad = results[1].reshape(row_count, feat_width)
    normed_low = results[2].reshape(row_count, feat_width)
    dprojected = results[3].reshape(row_count, 3 * feat_width)
    attended = results[4].reshape(row_count, feat_width)
    grad_terms = (contract(normed_low, dprojected, 0, 0), contract(attended, curve_grads, 0, 0))
    back_place = jnp.minimum(got_place, row_count - 1)
    back_rows = curve_out[back_place]
    back_grads = curve_grad[back_place]
    ret_rows, ret_grads = (
        lax.all_to_all(back_rows, ("sx", "sy"), split_axis=0, concat_axis=0, tiled=True),
        lax.all_to_all(back_grads, ("sx", "sy"), split_axis=0, concat_axis=0, tiled=True),
    )
    grad_sums = lax.psum((grad_terms[0], grad_terms[1]), ("sx", "sy"))
    grad_scale = 1.0 / math.sqrt(row_count * devices)
    return (
        ret_rows[slot_index],
        ret_grads[slot_index],
        grad_sums[0] * grad_scale,
        grad_sums[1] * grad_scale,
    )


def solution(mesh):
    in_specs = (P(("sx", "sy"), None), P(("sx", "sy"), None), P(("sx", "sy")), P(), P())
    out_specs = (P(("sx", "sy"), None), P(("sx", "sy"), None), P(), P())
    return jax.shard_map(
        on_device, mesh=mesh, in_specs=in_specs, out_specs=out_specs, check_vma=False
    )
```

profile of v0, /device:TPU:1, one launch (start us, length us, event | category | flops | bytes accessed | tf_op | source)
XLA Modules:
  0.0 736.6 jit_solution(12952684937199685522)
XLA Ops:
  7.2 5.1 sort.17
  13.2 4.5 gather_fusion
  18.6 4.3 scatter_custom_fusion
  22.9 4.3 scatter_custom_fusion.1
  27.9 11.5 %all-to-all-start = ((s32[128,16,1]{1,2,0:T(1,128)}), s32[128,16,1]{1,2,0:T(1,128)S(1)}, u32[]{:S(2)}, u32[]{:S(2)}) async-start(s32[128,16,1]{1,2,0:T(1,128)} %bitcast.6), calls=%async_computation | async-start | bytes 131072 | tf_op jit(solution)/shard_map/all_to_all | solution.py:104
  39.4 6.8 scatter_custom_fusion.2
  46.2 2.9 all-to-all-done
  49.8 6.8 all-to-all-start.1
  56.6 6.8 scatter_custom_fusion.4
  63.4 17.3 %all-to-all-done.1 = bf16[128,16,384]{2,1,0:T(8,128)(2,1)S(1)} async-done(((bf16[128,16,384]{2,1,0:T(8,128)(2,1)}), bf16[128,16,384]{2,1,0:T(8,128)(2,1)S(1)}, u32[]{:S(2)}, u32[]{:S(2)}) %all-to-all-start.1) | async-done | bytes 1572896 | tf_op jit(solution)/shard_map/all_to_all | solution.py:102
  81.8 4.9 all-to-all-start.2
  89.6 9.9 %scatter_custom_fusion.3 = bf16[1024,384]{1,0:T(8,128)(2,1)S(1)} fusion(s32[2048]{0:T(1024)} %bitcast.80, bf16[2048,384]{1,0:T(8,128)(2,1)} %bitcast.76, bf16[]{:T(256)} %constant.129.clone.1), kind=kCustom, calls=%fused_computation.78 | custom fusion | bytes 786944 | tf_op jit(solution)/shard_map/scatter | solution.py:107
  100.9 10.0 %all-to-all-done.2 = bf16[128,16,384]{2,1,0:T(8,128)(2,1)S(1)} async-done(((bf16[128,16,384]{2,1,0:T(8,128)(2,1)}), bf16[128,16,384]{2,1,0:T(8,128)(2,1)S(1)}, u32[]{:S(2)}, u32[]{:S(2)}) %all-to-all-start.2) | async-done | bytes 1572896 | tf_op jit(solution)/shard_map/all_to_all | solution.py:103
  112.1 9.9 %scatter_custom_fusion.5 = bf16[1024,384]{1,0:T(8,128)(2,1)S(1)} fusion(s32[2048]{0:T(1024)} %bitcast.81, bf16[2048,384]{1,0:T(8,128)(2,1)} %bitcast.75, bf16[]{:T(256)} %constant.129.clone.1), kind=kCustom, calls=%fused_computation.76 | custom fusion | bytes 786944 | tf_op jit(solution)/shard_map/scatter | solution.py:110
  122.7 3.7 convolution_convert_fusion.4
  126.9 391.0 %while.32 = (s32[]{:T(128)}, bf16[24,1024,16]{1,2,0:T(8,128)(2,1)}, bf16[24,1024,16]{1,2,0:T(8,128)(2,1)}, bf16[24,1024,16]{1,2,0:T(8,128)(2,1)}, bf16[24,1024,1...) while((s32[]{:T(128)}, bf16[24,1024,16]{1,2,0:T(8,128)(2,1)}, ...), condition=%wide.region_16.17_spmd, body=%wide.region_12.16_spmd.sunk | while | flops 227603472 | bytes 42127728 | solution.py:59
  132.9 2.5 fusion.96
  149.2 2.5 fusion.96
  165.5 2.5 fusion.96
  181.8 2.5 fusion.96
  230.7 2.5 fusion.96
  247.0 2.5 fusion.96
  263.3 2.5 fusion.96
  279.5 2.5 fusion.96
  328.4 2.5 fusion.96
  344.7 2.5 fusion.96
  361.0 2.5 fusion.96
  377.3 2.5 fusion.96
  393.6 2.5 fusion.96
  409.9 2.5 fusion.96
  426.2 2.5 fusion.96
  442.5 2.5 fusion.96
  458.8 2.5 fusion.96
  475.0 2.5 fusion.96
  491.3 2.5 fusion.96
  507.6 2.5 fusion.96
  519.7 9.0 %gather_fusion.1 = bf16[2048,384]{1,0:T(8,128)(2,1)} fusion(bf16[1024,384]{1,0:T(8,128)(2,1)S(1)} %fusion.41, s32[2048]{0:T(1024)S(1)} %broadcast_clamp_fusion), kind=kCustom, calls=%fused_computation.1 | custom fusion | bytes 3153920 | tf_op jit(solution)/shard_map/gather | solution.py:131
  528.8 5.0 all-to-all-start.3
  534.1 3.7 fusion.62
  537.8 3.1 copy.21
  540.9 2.9 fusion.63
  543.8 3.9 fusion.42
  551.8 9.0 %gather_fusion.3 = bf16[2048,384]{1,0:T(8,128)(2,1)} fusion(bf16[1024,384]{1,0:T(8,128)(2,1)S(1)} %fusion.39, s32[2048]{0:T(1024)S(1)} %broadcast_clamp_fusion), kind=kCustom, calls=%fused_computation.3 | custom fusion | bytes 3153920 | tf_op jit(solution)/shard_map/gather | solution.py:132
  560.8 10.3 %all-to-all-start.4 = ((bf16[128,16,384]{2,1,0:T(8,128)(2,1)}), bf16[128,16,384]{2,1,0:T(8,128)(2,1)}, u32[]{:S(2)}, u32[]{:S(2)}) async-start(bf16[128,16,384]{2,1,0:T(8,128)(2,1)} %bitcast.74), calls=%async_computation.4 | async-start | bytes 3145728 | tf_op jit(solution)/shard_map/all_to_all | solution.py:135
  571.1 142.4 %all-reduce.3.cloned.1.call-done = (f32[384,1152]{1,0:T(8,128)}, f32[384,384]{1,0:T(8,128)}) async-done(((f32[384,1152]{1,0:T(8,128)}, f32[384,384]{1,0:T(8,128)}), (f32[384,1152]{1,0:T(8,128)}, f32[384,384]{1,0:T(8,128)})) %all-reduce.3.cloned.1.call-update) | async-done | bytes 2359312 | tf_op jit(solution)/shard_map/psum | solution.py:137
  715.4 2.8 broadcast_multiply_fusion
  718.3 5.0 gather_fusion.2
  723.3 6.5 gather_fusion.4
  (260 shorter events, 343.2 us)
Async XLA Ops:
  7.2 115.5 %copy-start = (bf16[384,1152]{1,0:T(8,128)(2,1)S(1)}, bf16[384,1152]{1,0:T(8,128)(2,1)}, u32[]{:S(2)}) copy-start(bf16[384,1152]{1,0:T(8,128)(2,1)} %param.10) | copy-start | bytes 2654212
  27.9 21.2 %all-to-all-start = ((s32[128,16,1]{1,2,0:T(1,128)}), s32[128,16,1]{1,2,0:T(1,128)S(1)}, u32[]{:S(2)}, u32[]{:S(2)}) async-start(s32[128,16,1]{1,2,0:T(1,128)} %bitcast.6), calls=%async_computation | async-start | bytes 131072 | tf_op jit(solution)/shard_map/all_to_all | solution.py:104
  49.1 0.6 copy-start.9
  49.8 30.9 %all-to-all-start.1 = ((bf16[128,16,384]{2,1,0:T(8,128)(2,1)}), bf16[128,16,384]{2,1,0:T(8,128)(2,1)S(1)}, u32[]{:S(2)}, u32[]{:S(2)}) async-start(bf16[128,16,384]{2,1,0:T(8,128)(2,1)} %bitcast.8), calls=%async_computation.1 | async-start | bytes 3145728 | tf_op jit(solution)/shard_map/all_to_all | solution.py:102
  80.7 1.1 copy-start.7
  81.8 29.1 %all-to-all-start.2 = ((bf16[128,16,384]{2,1,0:T(8,128)(2,1)}), bf16[128,16,384]{2,1,0:T(8,128)(2,1)S(1)}, u32[]{:S(2)}, u32[]{:S(2)}) async-start(bf16[128,16,384]{2,1,0:T(8,128)(2,1)} %bitcast.10), calls=%async_computation.2 | async-start | bytes 3145728 | tf_op jit(solution)/shard_map/all_to_all | solution.py:103
  86.7 35.3 %copy-start.8 = (bf16[384,384]{1,0:T(8,128)(2,1)S(1)}, bf16[384,384]{1,0:T(8,128)(2,1)}, u32[]{:S(2)}) copy-start(bf16[384,384]{1,0:T(8,128)(2,1)} %param.11) | copy-start | bytes 884740
  99.6 418.3 %copy-start.1 = (bf16[1024,384]{1,0:T(8,128)(2,1)}, bf16[1024,384]{1,0:T(8,128)(2,1)S(1)}, u32[]{:S(2)}) copy-start(bf16[1024,384]{1,0:T(8,128)(2,1)S(1)} %scatter_custom_fusion.3) | copy-start | bytes 2359300
  110.9 1.1 copy-start.6
  122.0 4.3 copy-start.5
  528.8 5.3 copy-start.11
  528.8 32.0 %all-to-all-start.3 = ((bf16[128,16,384]{2,1,0:T(8,128)(2,1)}), bf16[128,16,384]{2,1,0:T(8,128)(2,1)S(1)}, u32[]{:S(2)}, u32[]{:S(2)}) async-start(bf16[128,16,384]{2,1,0:T(8,128)(2,1)} %bitcast.73), calls=%async_computation.3 | async-start | bytes 3145728 | tf_op jit(solution)/shard_map/all_to_all | solution.py:134
  533.8 179.7 %all-reduce.3.cloned.1.call-start = ((), (), s32[]{:S(2)}) async-start(), calls=%async_computation.5 | async-start | bytes 4718592 | tf_op jit(solution)/shard_map/psum | solution.py:137
  537.8 6.0 copy-start.2
  537.8 6.0 copy-start.10
  540.9 2.9 copy-start.12
  540.9 2.9 copy-start.13
  547.8 2.1 copy-start.3
  547.8 2.1 copy-start.4
  560.8 162.5 %all-to-all-start.4 = ((bf16[128,16,384]{2,1,0:T(8,128)(2,1)}), bf16[128,16,384]{2,1,0:T(8,128)(2,1)}, u32[]{:S(2)}, u32[]{:S(2)}) async-start(bf16[128,16,384]{2,1,0:T(8,128)(2,1)} %bitcast.74), calls=%async_computation.4 | async-start | bytes 3145728 | tf_op jit(solution)/shard_map/all_to_all | solution.py:135
Sparse Core Ops, SparseCore 0:
  547.9 165.5 all-reduce.2
where the time goes:
time: 741 us; the launch traced here: 737 us
  matrix products  314 us (42%)
  waiting for transfers between devices  173 us (23%)
  local copies, waits for them, and re-layouts  114 us (15%)
  other arithmetic  66.6 us (9%)
  starting transfers between devices  38.8 us (5%)
  loops' own time  16.7 us (2%)
  between operations  14.4 us (2%)
    dot_general x100, matrix products, contract(): lax.dot_general(left_op, right_op, (((left_dim,), (right_dim,)), ((), ())...  199 us
    psum x1, waiting for transfers between devices, on_device(): grad_sums = lax.psum((grad_terms[0], grad_terms[1]), ('sx', 'sy'))  142 us
    dot_general x24, matrix products, head_pass(): jnp.dot(prob_low, value_rows, preferred_element_type=jnp.float32)  59.7 us
    dot_general x24, matrix products, head_pass(): jnp.dot(dscores, key_rows, preferred_element_type=jnp.float32)  49.5 us
    convert_element_type x24, other arithmetic, head_pass(): dscores = (prob_full * (dprobs - jnp.sum(dprobs * prob_full, axis=1, keep...  30.2 us
    dynamic_slice x24, local copies, waits for them, and re-layouts, patch_pass(): heads_out = lax.map(one_head, jnp.arange(head_count, dtype=jnp.int32))  29.7 us
    scatter x2, local copies, waits for them, and re-layouts, on_device(): jnp.zeros((row_count, feat_width), jnp.bfloat16).at[got_place]  19.9 us
    reduce_sum x24, other arithmetic, head_pass(): prob_full = shifted / jnp.sum(shifted, axis=1, keepdims=True)  17.5 us
  transfers between devices with their start and end apart: 6, of which 4 were waited for; matrix products, arithmetic and copies ran while one was open for 9% of the time, Pallas kernels for 0%

commit v1 on v0

--- a/solution.py
+++ b/solution.py
@@ -134,7 +134,7 @@
         lax.all_to_all(back_rows, ("sx", "sy"), split_axis=0, concat_axis=0, tiled=True),
         lax.all_to_all(back_grads, ("sx", "sy"), split_axis=0, concat_axis=0, tiled=True),
     )
-    grad_sums = lax.psum((grad_terms[0], grad_terms[1]), ("sx", "sy"))
+    grad_sums = lax.psum(lax.psum((grad_terms[0], grad_terms[1]), "sx"), "sy")
     grad_scale = 1.0 / math.sqrt(row_count * devices)
     return (
         ret_rows[slot_index],

time: 741 us -> 712 us (0.961)
  local copies, waits for them, and re-layouts: 114 us -> 99 us
  waiting for transfers between devices: 173 us -> 161 us
    psum x1 -> x2, waiting for transfers between devices: 142 us -> 111 us  [on_device(): grad_sums = lax.psum(lax.psum((grad_terms[0], grad_terms[1]), 'sx'), 'sy')]
    all_to_all x1, waiting for transfers between devices: 0.01 us -> 19.6 us  [on_device(): lax.all_to_all(back_grads, ('sx', 'sy'), split_axis=0, concat_axis=0, til...]
    dynamic_slice x24, local copies, waits for them, and re-layouts: 29.7 us -> 14 us  [patch_pass(): heads_out = lax.map(one_head, jnp.arange(head_count, dtype=jnp.int32))]
  transfers between devices with their start and end apart: 6 -> 7, of which waited for: 4 -> 6; matrix products, arithmetic and copies ran while one was open for 9% -> 10% of each run, Pallas kernels for 0% -> 0%
where the time goes in v1:
time: 712 us; the launch traced here: 707 us
  matrix products  312 us (44%)
  waiting for transfers between devices  161 us (23%)
  local copies, waits for them, and re-layouts  99 us (14%)
  other arithmetic  65.1 us (9%)
  starting transfers between devices  38.7 us (5%)
  loops' own time  16.7 us (2%)
  between operations  14.4 us (2%)
    dot_general x100, matrix products, contract(): lax.dot_general(left_op, right_op, (((left_dim,), (right_dim,)), ((), ())...  199 us
    psum x2, waiting for transfers between devices, on_device(): grad_sums = lax.psum(lax.psum((grad_terms[0], grad_terms[1]), 'sx'), 'sy')  111 us
    dot_general x24, matrix products, head_pass(): jnp.dot(prob_low, value_rows, preferred_element_type=jnp.float32)  59.7 us
    dot_general x24, matrix products, head_pass(): jnp.dot(dscores, key_rows, preferred_element_type=jnp.float32)  49.5 us
    convert_element_type x24, other arithmetic, head_pass(): dscores = (prob_full * (dprobs - jnp.sum(dprobs * prob_full, axis=1, keep...  30.1 us
    scatter x2, local copies, waits for them, and re-layouts, on_device(): jnp.zeros((row_count, feat_width), jnp.bfloat16).at[got_place]  19.9 us
    all_to_all x1, waiting for transfers between devices, on_device(): lax.all_to_all(back_grads, ('sx', 'sy'), split_axis=0, concat_axis=0, til...  19.6 us
    reduce_sum x24, other arithmetic, head_pass(): prob_full = shifted / jnp.sum(shifted, axis=1, keepdims=True)  17.5 us
  transfers between devices with their start and end apart: 7, of which 6 were waited for; matrix products, arithmetic and copies ran while one was open for 10% of the time, Pallas kernels for 0%

profile of v1, /device:TPU:1, one launch (start us, length us, event | category | flops | bytes accessed | tf_op | source)
XLA Modules:
  0.0 706.7 jit_solution(4876388252102868747)
XLA Ops:
  7.2 5.1 sort.17
  13.2 4.5 gather_fusion
  18.6 4.3 scatter_custom_fusion
  22.9 4.3 scatter_custom_fusion.1
  27.9 11.5 %all-to-all-start = ((s32[128,16,1]{1,2,0:T(1,128)}), s32[128,16,1]{1,2,0:T(1,128)S(1)}, u32[]{:S(2)}, u32[]{:S(2)}) async-start(s32[128,16,1]{1,2,0:T(1,128)} %bitcast.6), calls=%async_computation | async-start | bytes 131072 | tf_op jit(solution)/shard_map/all_to_all | solution.py:104
  39.4 6.8 scatter_custom_fusion.2
  46.2 2.9 all-to-all-done
  49.8 6.8 all-to-all-start.1
  56.6 6.8 scatter_custom_fusion.4
  63.4 17.3 %all-to-all-done.1 = bf16[128,16,384]{2,1,0:T(8,128)(2,1)S(1)} async-done(((bf16[128,16,384]{2,1,0:T(8,128)(2,1)}), bf16[128,16,384]{2,1,0:T(8,128)(2,1)S(1)}, u32[]{:S(2)}, u32[]{:S(2)}) %all-to-all-start.1) | async-done | bytes 1572896 | tf_op jit(solution)/shard_map/all_to_all | solution.py:102
  81.8 4.9 all-to-all-start.2
  90.0 9.9 %scatter_custom_fusion.3 = bf16[1024,384]{1,0:T(8,128)(2,1)S(1)} fusion(s32[2048]{0:T(1024)} %bitcast.80, bf16[2048,384]{1,0:T(8,128)(2,1)} %bitcast.76, bf16[]{:T(256)} %constant.129.clone.1), kind=kCustom, calls=%fused_computation.78 | custom fusion | bytes 786944 | tf_op jit(solution)/shard_map/scatter | solution.py:107
  100.7 10.3 %all-to-all-done.2 = bf16[128,16,384]{2,1,0:T(8,128)(2,1)S(1)} async-done(((bf16[128,16,384]{2,1,0:T(8,128)(2,1)}), bf16[128,16,384]{2,1,0:T(8,128)(2,1)S(1)}, u32[]{:S(2)}, u32[]{:S(2)}) %all-to-all-start.2) | async-done | bytes 1572896 | tf_op jit(solution)/shard_map/all_to_all | solution.py:103
  112.1 9.9 %scatter_custom_fusion.5 = bf16[1024,384]{1,0:T(8,128)(2,1)S(1)} fusion(s32[2048]{0:T(1024)} %bitcast.81, bf16[2048,384]{1,0:T(8,128)(2,1)} %bitcast.75, bf16[]{:T(256)} %constant.129.clone.1), kind=kCustom, calls=%fused_computation.76 | custom fusion | bytes 786944 | tf_op jit(solution)/shard_map/scatter | solution.py:110
  122.7 3.0 convolution_convert_fusion.4
  125.7 375.3 %while.32 = (s32[]{:T(128)}, bf16[24,1024,16]{1,2,0:T(8,128)(2,1)}, bf16[24,1024,16]{1,2,0:T(8,128)(2,1)}, bf16[24,1024,16]{1,2,0:T(8,128)(2,1)}, bf16[24,1024,1...) while((s32[]{:T(128)}, bf16[24,1024,16]{1,2,0:T(8,128)(2,1)}, ...), condition=%wide.region_16.17_spmd, body=%wide.region_12.16_spmd.sunk | while | flops 227603472 | bytes 42127728 | solution.py:59
  131.1 2.5 fusion.96
  146.7 2.5 fusion.96
  162.3 2.5 fusion.96
  178.0 2.5 fusion.96
  193.6 2.5 fusion.96
  209.2 2.5 fusion.96
  224.9 2.5 fusion.96
  240.5 2.5 fusion.96
  287.4 2.5 fusion.96
  303.1 2.5 fusion.96
  334.3 2.5 fusion.96
  350.0 2.5 fusion.96
  365.6 2.5 fusion.96
  381.3 2.5 fusion.96
  428.2 2.5 fusion.96
  443.8 2.5 fusion.96
  475.1 2.5 fusion.96
  490.7 2.5 fusion.96
  501.0 2.6 fusion.63
  503.7 3.9 fusion.42
  509.4 9.0 %gather_fusion.1 = bf16[2048,384]{1,0:T(8,128)(2,1)} fusion(bf16[1024,384]{1,0:T(8,128)(2,1)S(1)} %fusion.41, s32[2048]{0:T(1024)S(1)} %broadcast_clamp_fusion), kind=kCustom, calls=%fused_computation.1 | custom fusion | bytes 3153920 | tf_op jit(solution)/shard_map/gather | solution.py:131
  518.5 5.0 all-to-all-start.3
  523.6 3.7 fusion.62
  527.3 3.1 copy.21
  530.4 54.1 %all-reduce.7.cloned.1.call-done = (f32[384,1152]{1,0:T(8,128)}, f32[384,384]{1,0:T(8,128)}) async-done(((f32[384,1152]{1,0:T(8,128)}, f32[384,384]{1,0:T(8,128)}), (f32[384,1152]{1,0:T(8,128)}, f32[384,384]{1,0:T(8,128)})) %all-reduce.7.cloned.1.call-update) | async-done | bytes 2359312 | tf_op jit(solution)/shard_map/psum | solution.py:137
  588.6 9.1 %gather_fusion.3 = bf16[2048,384]{1,0:T(8,128)(2,1)} fusion(bf16[1024,384]{1,0:T(8,128)(2,1)S(1)} %fusion.39, s32[2048]{0:T(1024)S(1)} %broadcast_clamp_fusion), kind=kCustom, calls=%fused_computation.3 | custom fusion | bytes 3153920 | tf_op jit(solution)/shard_map/gather | solution.py:132
  597.7 10.2 %all-to-all-start.4 = ((bf16[128,16,384]{2,1,0:T(8,128)(2,1)}), bf16[128,16,384]{2,1,0:T(8,128)(2,1)}, u32[]{:S(2)}, u32[]{:S(2)}) async-start(bf16[128,16,384]{2,1,0:T(8,128)(2,1)} %bitcast.74), calls=%async_computation.4 | async-start | bytes 3145728 | tf_op jit(solution)/shard_map/all_to_all | solution.py:135
  607.9 5.0 gather_fusion.2
  612.9 19.6 %all-to-all-done.4 = bf16[128,16,384]{2,1,0:T(8,128)(2,1)} async-done(((bf16[128,16,384]{2,1,0:T(8,128)(2,1)}), bf16[128,16,384]{2,1,0:T(8,128)(2,1)}, u32[]{:S(2)}, u32[]{:S(2)}) %all-to-all-start.4) | async-done | bytes 1572896 | tf_op jit(solution)/shard_map/all_to_all | solution.py:135
  632.5 6.5 gather_fusion.4
  639.0 57.1 %all-reduce.5.cloned.1.call-done = (f32[384,1152]{1,0:T(8,128)}, f32[384,384]{1,0:T(8,128)}) async-done(((f32[384,1152]{1,0:T(8,128)}, f32[384,384]{1,0:T(8,128)}), (f32[384,1152]{1,0:T(8,128)}, f32[384,384]{1,0:T(8,128)})) %all-reduce.5.cloned.1.call-update) | async-done | bytes 2359312 | tf_op jit(solution)/shard_map/psum | solution.py:137
  696.1 2.9 broadcast_multiply_fusion
  (271 shorter events, 330.5 us)
Async XLA Ops:
  7.2 115.5 %copy-start = (bf16[384,1152]{1,0:T(8,128)(2,1)S(1)}, bf16[384,1152]{1,0:T(8,128)(2,1)}, u32[]{:S(2)}) copy-start(bf16[384,1152]{1,0:T(8,128)(2,1)} %param.10) | copy-start | bytes 2654212
  27.9 21.2 %all-to-all-start = ((s32[128,16,1]{1,2,0:T(1,128)}), s32[128,16,1]{1,2,0:T(1,128)S(1)}, u32[]{:S(2)}, u32[]{:S(2)}) async-start(s32[128,16,1]{1,2,0:T(1,128)} %bitcast.6), calls=%async_computation | async-start | bytes 131072 | tf_op jit(solution)/shard_map/all_to_all | solution.py:104
  49.1 0.6 copy-start.11
  49.8 30.9 %all-to-all-start.1 = ((bf16[128,16,384]{2,1,0:T(8,128)(2,1)}), bf16[128,16,384]{2,1,0:T(8,128)(2,1)S(1)}, u32[]{:S(2)}, u32[]{:S(2)}) async-start(bf16[128,16,384]{2,1,0:T(8,128)(2,1)} %bitcast.8), calls=%async_computation.1 | async-start | bytes 3145728 | tf_op jit(solution)/shard_map/all_to_all | solution.py:102
  80.7 1.1 copy-start.7
  81.8 29.1 %all-to-all-start.2 = ((bf16[128,16,384]{2,1,0:T(8,128)(2,1)}), bf16[128,16,384]{2,1,0:T(8,128)(2,1)S(1)}, u32[]{:S(2)}, u32[]{:S(2)}) async-start(bf16[128,16,384]{2,1,0:T(8,128)(2,1)} %bitcast.10), calls=%async_computation.2 | async-start | bytes 3145728 | tf_op jit(solution)/shard_map/all_to_all | solution.py:103
  86.7 35.3 %copy-start.10 = (bf16[384,384]{1,0:T(8,128)(2,1)S(1)}, bf16[384,384]{1,0:T(8,128)(2,1)}, u32[]{:S(2)}) copy-start(bf16[384,384]{1,0:T(8,128)(2,1)} %param.11) | copy-start | bytes 884740
  86.7 497.8 %all-reduce.7.cloned.1.call-start = ((), (), s32[]{:S(2)}) async-start(), calls=%async_computation.6 | async-start | bytes 4718592 | tf_op jit(solution)/shard_map/psum | solution.py:137
  100.0 408.3 %copy-start.1 = (bf16[1024,384]{1,0:T(8,128)(2,1)}, bf16[1024,384]{1,0:T(8,128)(2,1)S(1)}, u32[]{:S(2)}) copy-start(bf16[1024,384]{1,0:T(8,128)(2,1)S(1)} %scatter_custom_fusion.3) | copy-start | bytes 2359300
  100.7 403.0 %copy-start.12 = (f32[1024]{0:T(1024)}, f32[1024]{0:T(1024)S(1)}, u32[]{:S(2)}) copy-start(f32[1024]{0:T(1024)S(1)} %add_rsqrt_fusion) | copy-start | bytes 12292
  110.9 1.1 copy-start.6
  122.0 379.0 %copy-start.5 = (bf16[1024,384]{1,0:T(8,128)(2,1)}, bf16[1024,384]{1,0:T(8,128)(2,1)S(1)}, u32[]{:S(2)}) copy-start(bf16[1024,384]{1,0:T(8,128)(2,1)S(1)} %scatter_custom_fusion.5) | copy-start | bytes 2359300
  501.0 2.6 copy-start.15
  501.0 2.6 copy-start.17
  507.6 0.7 copy-start.14
  507.6 1.1 copy-start.8
  518.5 5.1 copy-start.16
  518.5 79.2 %all-to-all-start.3 = ((bf16[128,16,384]{2,1,0:T(8,128)(2,1)}), bf16[128,16,384]{2,1,0:T(8,128)(2,1)S(1)}, u32[]{:S(2)}, u32[]{:S(2)}) async-start(bf16[128,16,384]{2,1,0:T(8,128)(2,1)} %bitcast.73), calls=%async_computation.3 | async-start | bytes 3145728 | tf_op jit(solution)/shard_map/all_to_all | solution.py:134
  523.5 172.5 %all-reduce.5.cloned.1.call-start = ((), (), s32[]{:S(2)}) async-start(), calls=%async_computation.5 | async-start | bytes 4718592 | tf_op jit(solution)/shard_map/psum | solution.py:137
  527.3 57.3 %copy-start.2 = (bf16[1024,384]{1,0:T(8,128)(2,1)S(1)}, bf16[1024,384]{1,0:T(8,128)(2,1)}, u32[]{:S(2)}) copy-start(bf16[1024,384]{1,0:T(8,128)(2,1)} %copy-done.1) | copy-start | bytes 2359300
  527.3 57.3 %copy-start.13 = (f32[1024]{0:T(1024)S(1)}, f32[1024]{0:T(1024)}, u32[]{:S(2)}) copy-start(f32[1024]{0:T(1024)} %copy-done.12) | copy-start | bytes 12292
  584.6 2.1 copy-start.3
  584.6 2.1 copy-start.4
  597.7 34.8 %all-to-all-start.4 = ((bf16[128,16,384]{2,1,0:T(8,128)(2,1)}), bf16[128,16,384]{2,1,0:T(8,128)(2,1)}, u32[]{:S(2)}, u32[]{:S(2)}) async-start(bf16[128,16,384]{2,1,0:T(8,128)(2,1)} %bitcast.74), calls=%async_computation.4 | async-start | bytes 3145728 | tf_op jit(solution)/shard_map/all_to_all | solution.py:135
  696.1 2.9 copy-start.9
Sparse Core Ops, SparseCore 0:
  507.7 76.7 all-reduce.6
  588.0 108.0 all-reduce.4
